TPU v7x, 32 devices: a whole 2x2x4 slice. The times are simulated.
32 devices in a mesh: loop: 16 (over z, y, core), narrow: 2 (over x).
Axes of the slice: x: 2, y: 2, z: 4, core: 2. Of those that a mesh axis runs over, the one named last changes fastest.
Arguments:
- queries: bfloat16 [8192, 4096], P(('loop', 'narrow')), may hold values from -2 to 2
- passages: bfloat16 [64, 4096], P('loop'), may hold values from -10 to 10
- pos_ids: int32 [8192], P(('loop', 'narrow')), may hold values from 0 to 63
- neg_ids: int32 [8192, 32], P(('loop', 'narrow')), may hold values from 0 to 63
- neg_mask: int32 [8192, 32], P(('loop', 'narrow')), may hold values 0 or 1
- neg_counts: int32 [8192], P(('loop', 'narrow')), may hold values from 0 to 32
- d_loss: float32 [8192], P(('loop', 'narrow')), may hold values from -6 to 6
Outputs:
- query_loss: float32 [8192], P(('loop', 'narrow'))
- grad_queries: bfloat16 [8192, 4096], P(('loop', 'narrow'))
- grad_passages: bfloat16 [64, 4096], P('loop')
Inputs may be any that keep to these rules, and one draw needn't show every extreme that they name: `neg_counts`: slots at or beyond a query's count are padding.
All inputs are finite; a program needn't handle non-finite values. No bound on the sum of `neg_mask` on one device may be relied on, other than what follows from the above.
Results may differ from a plain program's by a relative error of at most 0.0058.
Values may be sent and summed in bfloat16 or wider, within the bound.
No kernel may reach another device: no remote copies, remote signals or barrier semaphores. Data moves between devices by JAX's collectives and lax.ppermute only.
A program may use at most 64 MiB of HBM per device.

v0:
```python
import jax
import jax.numpy as jnp
from jax import lax
from jax.sharding import PartitionSpec as P

NEG = 32
logit_scale = 50.0
norm_eps = 1e-06


def normalize(rows):
    wide = rows.astype(jnp.float32)
    scales = lax.rsqrt(jnp.sum(wide * wide, axis=-1) + norm_eps)
    return (scales, (wide * scales[:, None]).astype(jnp.bfloat16))


def weight_table(valid, neg_ids, pool_size):
    columns = jnp.arange(pool_size, dtype=jnp.int32)
    weights = jnp.ones((neg_ids.shape[0], pool_size), jnp.float32)
    for first in range(0, NEG, 8):
        named = neg_ids[:, first : first + 8]
        usable = valid[:, first : first + 8]
        hits = (named[:, :, None] == columns[None, None, :]) & usable[:, :, None]
        weights = weights + jnp.sum(hits.astype(jnp.float32), axis=1)
    return weights


def tangent_back(rows, scales, direction):
    unit = rows.astype(jnp.float32) * scales[:, None]
    inner = jnp.sum(unit * direction, axis=-1, keepdims=True)
    return (scales[:, None] * (direction - unit * inner)).astype(jnp.bfloat16)


def local(queries, passages, pos_ids, neg_ids, neg_mask, neg_counts, d_loss):
    qscale, qnorm = normalize(queries)
    pscale, pnorm = normalize(passages)
    pool = lax.all_gather(pnorm, "loop", axis=0, tiled=True)
    pool_size = pool.shape[0]
    columns = jnp.arange(pool_size, dtype=jnp.int32)
    slots = jnp.arange(NEG, dtype=jnp.int32)
    scores = logit_scale * lax.dot_general(
        qnorm, pool, (((1,), (1,)), ((), ())), preferred_element_type=jnp.float32
    )
    valid = (neg_mask == 1) & (slots[None, :] < neg_counts[:, None])
    weights = weight_table(valid, neg_ids, pool_size)
    terms = weights * jnp.exp(scores)
    denom = jnp.sum(terms, axis=1)
    chosen = columns[None, :] == pos_ids[:, None]
    picked = jnp.sum(jnp.where(chosen, scores, 0.0), axis=1)
    query_loss = jnp.log(denom) - picked
    coef = (
        logit_scale * d_loss[:, None] * (terms / denom[:, None] - chosen.astype(jnp.float32))
    ).astype(jnp.bfloat16)
    qdir = jnp.dot(coef, pool, preferred_element_type=jnp.float32)
    grad_queries = tangent_back(queries, qscale, qdir)
    partial_dir = lax.psum_scatter(
        lax.dot_general(coef, qnorm, (((0,), (0,)), ((), ())), preferred_element_type=jnp.float32),
        "loop",
        scatter_dimension=0,
        tiled=True,
    )
    pdir = lax.psum(partial_dir, "narrow")
    grad_passages = tangent_back(passages, pscale, pdir)
    return (query_loss, grad_queries, grad_passages)


def solution(mesh):
    return jax.shard_map(
        local,
        mesh=mesh,
        in_specs=(
            P(("loop", "narrow"), None),
            P("loop", None),
            P(("loop", "narrow")),
            P(("loop", "narrow"), None),
            P(("loop", "narrow"), None),
            P(("loop", "narrow")),
            P(("loop", "narrow")),
        ),
        out_specs=(P(("loop", "narrow")), P(("loop", "narrow"), None), P("loop", None)),
        check_vma=False,
    )
```

profile of v0, /device:TPU:0, one launch (start us, length us, event | category | flops | bytes accessed | tf_op | source)
XLA Modules:
  0.0 164.1 jit_solution(8291174964269630213)
XLA Ops:
  7.2 0.0 copy-start
  7.2 0.0 copy-start.2
  7.2 0.0 all-reduce.6.cloned.1.call-start
  7.2 1.0 fusion.22
  8.3 2.1 %fusion.7 = f32[256]{0:T(256)S(1)} fusion(bf16[256,4096]{1,0:T(8,128)(2,1)} %param.7), kind=kLoop, calls=%fused_computation.9 | loop fusion | flops 3145472 | bytes 2098176 | tf_op jit(solution)/shard_map/reduce_sum | solution.py:13
  10.4 0.8 fusion.24
  11.2 0.8 fusion.23
  12.0 0.8 fusion.27
  12.8 24.6 %all-gather = bf16[16,4,4096]{2,1,0:T(4,128)(2,1)S(1)} all-gather(bf16[1,4,4096]{2,1,0:T(4,128)(2,1)S(1)} %fusion.23), channel_id=1, replica_groups=mesh['loop'=16,'narrow'=2] {'loop'}, dimensions={0}, use_global_device_ids=true | all-gather | bytes 557056 | tf_op jit(solution)/shard_map/all_gather | solution.py:37
  37.4 0.1 reshape.30
  37.5 0.7 add_rsqrt_fusion
  38.2 0.2 convert_reduce_fusion.2
  38.4 0.2 convert_reduce_fusion
  38.6 0.0 copy-done
  38.6 0.0 copy-done.2
  38.6 0.9 fusion.26
  39.4 1.7 %fusion.8 = f32[64,4096]{1,0:T(8,128)} fusion(bf16[256,4096]{1,0:T(8,128)(2,1)S(1)} %copy-done, f32[256]{0:T(256)S(1)} %get-tuple-element.20, f32[256,64]{0,1:T(8,128)S(1)} %get-tuple-element.4, f32[256]{0:T(256)S(1)} %get-tuple-element.3, f32[256]{0:T(256)S(1)} %get-tuple-element.21, s32[256]{0:T(256)S(1)} %copy-done.2), kind=kOutput, calls=%fused_computation.11 | convolution fusion | flops 137461760 | bytes 3215360 | tf_op jit(solution)/shard_map/dot_general | solution.py:57
  41.1 0.0 all-reduce.6.cloned.1.call-update
  41.1 0.0 all-reduce.4.cloned.1.call-start
  41.2 0.9 fusion.3
  42.1 0.0 copy-start.3
  42.1 0.0 copy-start.1
  42.1 2.5 %fusion.6 = bf16[256,4096]{1,0:T(8,128)(2,1)} fusion(f32[256,4096]{1,0:T(8,128)S(1)} %get-tuple-element.15, bf16[256,4096]{1,0:T(8,128)(2,1)S(1)} %copy-done, f32[256]{0:T(256)S(1)} %get-tuple-element.14, f32[256]{0:T(256)S(1)} %get-tuple-element.20), kind=kLoop, calls=%fused_computation.8 | loop fusion | flops 6291456 | bytes 8390656 | tf_op jit(solution)/shard_map/convert_element_type | solution.py:31
  44.6 0.0 copy-done.3
  44.6 0.6 dynamic-slice
  45.8 86.6 %all-reduce.6.cloned.1.call-done = f32[64,4096]{1,0:T(8,128)} async-done(((f32[64,4096]{1,0:T(8,128)}), f32[64,4096]{1,0:T(8,128)}) %all-reduce.6.cloned.1.call-update) | async-done | bytes 1048592
  132.4 1.5 constant_dynamic-slice_fusion
  133.9 0.0 all-reduce.4.cloned.1.call-update
  133.9 0.6 log_subtract_fusion
  134.5 20.2 %all-reduce.4.cloned.1.call-done = f32[4,4096]{1,0:T(4,128)} async-done(((f32[4,4096]{1,0:T(4,128)}), f32[4,4096]{1,0:T(4,128)}) %all-reduce.4.cloned.1.call-update) | async-done | bytes 65552 | tf_op jit(solution)/shard_map/psum | solution.py:62
  154.7 0.0 copy-done.1
  154.7 1.1 fusion.18
  155.7 1.5 fusion.21
  (2 shorter events, 0.0 us)
Async XLA Ops:
  7.2 31.4 %copy-start = (bf16[256,4096]{1,0:T(8,128)(2,1)S(1)}, bf16[256,4096]{1,0:T(8,128)(2,1)}, u32[]{:S(2)}) copy-start(bf16[256,4096]{1,0:T(8,128)(2,1)} %param.7) | copy-start | bytes 6291460
  7.2 31.4 %copy-start.2 = (s32[256]{0:T(256)S(1)}, s32[256]{0:T(256)}, u32[]{:S(2)}) copy-start(s32[256]{0:T(256)} %param.9) | copy-start | bytes 3076
  7.2 125.2 %all-reduce.6.cloned.1.call-start = ((), (), s32[]{:S(2)}) async-start(), calls=%async_computation.1 | async-start | bytes 2097152
  41.1 113.5 %all-reduce.4.cloned.1.call-start = ((), (), s32[]{:S(2)}) async-start(), calls=%async_computation | async-start | bytes 131072 | tf_op jit(solution)/shard_map/psum | solution.py:62
  42.1 2.5 %copy-start.3 = (u32[32]{0:T(128)S(1)}, u32[32]{0:T(128)}, u32[]{:S(2)}) copy-start(u32[32]{0:T(128)} %constant.15) | copy-start | bytes 388
  42.1 112.6 %copy-start.1 = (bf16[4,4096]{1,0:T(4,128)(2,1)S(1)}, bf16[4,4096]{1,0:T(4,128)(2,1)}, u32[]{:S(2)}) copy-start(bf16[4,4096]{1,0:T(4,128)(2,1)} %param.8) | copy-start | bytes 98308
Sparse Core Ops, SparseCore 0:
  41.3 91.0 all-reduce.5
  134.6 20.0 all-reduce.3
where the time goes:
time: 165 us; the launch traced here: 164 us
  waiting for transfers between devices  107 us (65%)
  blocking collectives  24.6 us (15%)
  between operations  14.8 us (9%)
  other arithmetic  11.5 us (7%)
  matrix products  3.43 us (2%)
  local copies, waits for them, and re-layouts  3.01 us (2%)
    unnamed x3, waiting for transfers between devices  86.6 us
    all_gather x1, blocking collectives, local(): pool = lax.all_gather(pnorm, 'loop', axis=0, tiled=True)  24.6 us
    psum x1, waiting for transfers between devices, local(): pdir = lax.psum(partial_dir, 'narrow')  20.2 us
    convert_element_type x2, other arithmetic, tangent_back(): return (scales[:, None] * (direction - unit * inner)).astype(jnp.bfloat16)  4.01 us
  transfers between devices with their start and end apart: 2, of which 2 were waited for; matrix products, arithmetic and copies ran while one was open for 3% of the time, Pallas kernels for 0%

commit v1 on v0

--- a/solution.py
+++ b/solution.py
@@ -6,6 +6,10 @@
 NEG = 32
 logit_scale = 50.0
 norm_eps = 1e-06
+
+
+def _obtain_ends(shard_in, bus_axis):
+    return jnp.sum(lax.all_gather(shard_in, bus_axis), 0)
 
 
 def normalize(rows):
@@ -59,7 +63,7 @@
         scatter_dimension=0,
         tiled=True,
     )
-    pdir = lax.psum(partial_dir, "narrow")
+    pdir = _obtain_ends(partial_dir, "narrow")
     grad_passages = tangent_back(passages, pscale, pdir)
     return (query_loss, grad_queries, grad_passages)
 

time: 165 us -> 146 us (0.88)
  waiting for transfers between devices: 107 us -> 86 us
  blocking collectives: 24.6 us -> 29.5 us
  other arithmetic: 11.5 us -> 9.83 us
    psum x1 -> x0, waiting for transfers between devices: 20.2 us -> none  [local(): pdir = lax.psum(partial_dir, 'narrow')]
    all_gather x0 -> x1, blocking collectives: none -> 4.93 us  [_obtain_ends(): return jnp.sum(lax.all_gather(shard_in, bus_axis), 0)]
    unnamed x3 -> x2, waiting for transfers between devices: 86.6 us -> 86 us
  transfers between devices with their start and end apart: 2 -> 1, of which waited for: 2 -> 1; matrix products, arithmetic and copies ran while one was open for 3% -> 3% of each run, Pallas kernels for 0% -> 0%
where the time goes in v1:
time: 146 us
  waiting for transfers between devices  86 us (59%)
  blocking collectives  29.5 us (20%)
  between operations  14.8 us (10%)
  other arithmetic  9.83 us (7%)
  matrix products  3.47 us (2%)
  local copies, waits for them, and re-layouts  2.4 us (2%)
    unnamed x2, waiting for transfers between devices  86 us
    all_gather x1, blocking collectives, local(): pool = lax.all_gather(pnorm, 'loop', axis=0, tiled=True)  24.6 us
    all_gather x1, blocking collectives, _obtain_ends(): return jnp.sum(lax.all_gather(shard_in, bus_axis), 0)  4.93 us
    convert_element_type x2, other arithmetic, tangent_back(): return (scales[:, None] * (direction - unit * inner)).astype(jnp.bfloat16)  3.18 us
    reduce_sum x2, other arithmetic, normalize(): scales = lax.rsqrt(jnp.sum(wide * wide, axis=-1) + norm_eps)  3.13 us
  transfers between devices with their start and end apart: 1, of which 1 were waited for; matrix products, arithmetic and copies ran while one was open for 3% of the time, Pallas kernels for 0%

profile of v1, /device:TPU:0, one launch (start us, length us, event | category | flops | bytes accessed | tf_op | source)
XLA Modules:
  0.0 146.1 jit_solution(2441135998431496281)
XLA Ops:
  7.2 0.0 copy-start
  7.2 0.0 copy-start.2
  7.2 0.0 all-reduce.3.cloned.1.call-start
  7.2 1.0 fusion.22
  8.3 2.1 %fusion.7 = f32[256]{0:T(256)S(1)} fusion(bf16[256,4096]{1,0:T(8,128)(2,1)} %param.7), kind=kLoop, calls=%fused_computation.9 | loop fusion | flops 3145472 | bytes 2098176 | tf_op jit(solution)/shard_map/reduce_sum | solution.py:17
  10.4 0.8 fusion.24
  11.2 0.8 fusion.23
  12.0 0.8 fusion.27
  12.8 24.6 %all-gather.1 = bf16[16,4,4096]{2,1,0:T(4,128)(2,1)S(1)} all-gather(bf16[1,4,4096]{2,1,0:T(4,128)(2,1)S(1)} %fusion.23), channel_id=1, replica_groups=mesh['loop'=16,'narrow'=2] {'loop'}, dimensions={0}, use_global_device_ids=true | all-gather | bytes 557056 | tf_op jit(solution)/shard_map/all_gather | solution.py:41
  37.4 0.1 reshape.31
  37.5 0.7 add_rsqrt_fusion
  38.2 0.2 convert_reduce_fusion.2
  38.4 0.2 convert_reduce_fusion
  38.6 0.0 copy-done
  38.6 0.0 copy-done.2
  38.6 0.9 fusion.26
  39.4 1.7 %fusion.8 = f32[64,4096]{1,0:T(8,128)} fusion(bf16[256,4096]{1,0:T(8,128)(2,1)S(1)} %copy-done, f32[256]{0:T(256)S(1)} %get-tuple-element.20, f32[256,64]{0,1:T(8,128)S(1)} %get-tuple-element.4, f32[256]{0:T(256)S(1)} %get-tuple-element.3, f32[256]{0:T(256)S(1)} %get-tuple-element.21, s32[256]{0:T(256)S(1)} %copy-done.2), kind=kOutput, calls=%fused_computation.11 | convolution fusion | flops 137461760 | bytes 3215360 | tf_op jit(solution)/shard_map/dot_general | solution.py:61
  41.1 0.0 all-reduce.3.cloned.1.call-update
  41.1 0.9 fusion.3
  42.1 0.0 copy-start.3
  42.1 0.0 copy-start.1
  42.1 2.5 %fusion.6 = bf16[256,4096]{1,0:T(8,128)(2,1)} fusion(f32[256,4096]{1,0:T(8,128)S(1)} %get-tuple-element.15, bf16[256,4096]{1,0:T(8,128)(2,1)S(1)} %copy-done, f32[256]{0:T(256)S(1)} %get-tuple-element.14, f32[256]{0:T(256)S(1)} %get-tuple-element.20), kind=kLoop, calls=%fused_computation.8 | loop fusion | flops 6291456 | bytes 8390656 | tf_op jit(solution)/shard_map/convert_element_type | solution.py:35
  44.6 0.0 copy-done.3
  44.6 0.6 dynamic-slice
  45.8 0.6 log_subtract_fusion
  46.4 86.0 %all-reduce.3.cloned.1.call-done = f32[64,4096]{1,0:T(8,128)} async-done(((f32[64,4096]{1,0:T(8,128)}), f32[64,4096]{1,0:T(8,128)}) %all-reduce.3.cloned.1.call-update) | async-done | bytes 1048592
  132.4 0.9 dynamic-slice_bitcast_fusion
  133.3 4.9 %all-gather.2 = f32[2,4,4096]{2,1,0:T(4,128)S(1)} all-gather(f32[1,4,4096]{2,1,0:T(4,128)S(1)} %dynamic-slice_bitcast_fusion), channel_id=2, replica_groups=mesh['loop'=16,'narrow'=2] {'narrow'}, dimensions={0}, use_global_device_ids=true | all-gather | bytes 196608 | tf_op jit(solution)/shard_map/all_gather | solution.py:12
  138.3 0.0 copy-done.1
  138.3 0.2 fusion.18
  138.5 0.7 fusion.21
  (3 shorter events, 0.0 us)
Async XLA Ops:
  7.2 31.4 %copy-start = (bf16[256,4096]{1,0:T(8,128)(2,1)S(1)}, bf16[256,4096]{1,0:T(8,128)(2,1)}, u32[]{:S(2)}) copy-start(bf16[256,4096]{1,0:T(8,128)(2,1)} %param.7) | copy-start | bytes 6291460
  7.2 31.4 %copy-start.2 = (s32[256]{0:T(256)S(1)}, s32[256]{0:T(256)}, u32[]{:S(2)}) copy-start(s32[256]{0:T(256)} %param.9) | copy-start | bytes 3076
  7.2 125.2 %all-reduce.3.cloned.1.call-start = ((), (), s32[]{:S(2)}) async-start(), calls=%async_computation | async-start | bytes 2097152
  42.1 2.5 %copy-start.3 = (u32[32]{0:T(128)S(1)}, u32[32]{0:T(128)}, u32[]{:S(2)}) copy-start(u32[32]{0:T(128)} %constant.15) | copy-start | bytes 388
  42.1 96.2 %copy-start.1 = (bf16[4,4096]{1,0:T(4,128)(2,1)S(1)}, bf16[4,4096]{1,0:T(4,128)(2,1)}, u32[]{:S(2)}) copy-start(bf16[4,4096]{1,0:T(4,128)(2,1)} %param.8) | copy-start | bytes 98308
Sparse Core Ops, SparseCore 0:
  41.3 91.0 all-reduce.2
